TPU v7x, 256 devices: a whole 4x4x8 slice. The times are simulated.
256 devices in a mesh: sector: 16 (over y, x_hi, core), depth: 16 (over x_lo, z).
Axes of the slice: x: 4 (x_hi: 2, x_lo: 2; x = x_hi * 2 + x_lo), y: 4, z: 8, core: 2. Of those that a mesh axis runs over, the one named last changes fastest.
Arguments:
- panel: bfloat16 [1048576, 128], P(('sector', 'depth')), may hold values from -6 to 6
- coords: int32 [3, 1048576], P(None, ('sector', 'depth')), may hold values from 0 to 127, as said below
- neighbours: int32 [8192, 32], P(('sector', 'depth')), may hold values from 0 to 8191, as said below
- ranges: float32 [3], replicated, may hold values from 6 to 20
Outputs:
- basis: float32 [1048576, 128], P(('sector', 'depth'))
- factor: float32 [128, 128], replicated
Inputs may be any that keep to these rules, and one draw needn't show every extreme that they name: `coords`: each device's 32 * 128 cells occupy every point of its own grid box exactly once: azimuth columns s * 8 to (s + 1) * 8 - 1 for sector s, radial rows 0 to 63, depth layers d * 8 to (d + 1) * 8 - 1 for slab d, in an arbitrary order; cell blocks are numbered sector-major, then slab, then block. `neighbours`: each row lists 32 different block columns, all of the row's depth slab and of sectors at most two away from its own around the cycle.
All inputs are finite; a program needn't handle non-finite values.
Results may differ from a plain program's by a relative error of at most 0.0065.
Values may be sent and summed in bfloat16 or wider, within the bound.
A program may use at most 128 MiB of HBM per device.

v0:
```python
import jax
import jax.numpy as jnp
from jax import lax
from jax.sharding import PartitionSpec as P

AZ_SEC = 8
CUTOFF = 3.0
NUGGET = 0.5


def passed_along(block, axis, distance):
    devices = range(lax.axis_size(axis))
    route = [((i - distance) % len(devices), i) for i in devices]
    return lax.ppermute(block, axis, route)


def as_sent(value):

    def short(part):
        return part.astype(jnp.bfloat16) if part.dtype == jnp.float32 else part

    return jax.tree.map(short, value)


def cov_blocks(home, remote, ranges, period):
    diffs = (home[:, None, :, :, None] - remote[:, :, :, None, :]).astype(jnp.float32)
    along = jnp.abs(diffs[:, :, 0])
    along = jnp.minimum(along, period - along)
    scaled = (
        (along / ranges[0]) ** 2
        + (diffs[:, :, 1] / ranges[1]) ** 2
        + (diffs[:, :, 2] / ranges[2]) ** 2
    )
    radius = jnp.sqrt(scaled)
    taper = jnp.maximum(1.0 - radius / CUTOFF, 0.0)
    weight = 8.0 / jnp.sqrt(jnp.float32(remote.shape[1] * remote.shape[3]))
    return (weight * jnp.exp(-radius) * taper * taper).astype(jnp.bfloat16)


def on_device(panel, coords, neighbours, ranges):
    block_count = neighbours.shape[0]
    block_size = panel.shape[0] // block_count
    width = panel.shape[1]
    sector_count = lax.axis_size("sector")
    slab_count = lax.axis_size("depth")
    my_sector = lax.axis_index("sector")
    blocked = panel.reshape(block_count, block_size, width)
    near_side = {}
    far_side = {}
    for direction in (1, -1):
        near_side[direction] = passed_along((blocked, coords), "sector", direction)
    for direction in (1, -1):
        far_side[direction] = passed_along(
            (near_side[direction][0], as_sent(near_side[direction][1])), "sector", direction
        )
    ordered = [far_side[1], near_side[1], (blocked, coords), near_side[-1], far_side[-1]]
    wide_panel = jnp.concatenate([member[0] for member in ordered], axis=0)
    wide_coords = jnp.concatenate(
        [member[1].reshape(3, block_count, block_size) for member in ordered], axis=1
    )
    wide_coords = jnp.transpose(wide_coords, (1, 0, 2))
    home_coords = jnp.transpose(coords.reshape(3, block_count, block_size), (1, 0, 2))
    column_sector = neighbours // (slab_count * block_count)
    step_away = (column_sector - my_sector + 2) % sector_count
    local_column = step_away * block_count + neighbours % block_count
    period = jnp.float32(AZ_SEC * sector_count)
    group = 4
    turns = block_count // group

    def one_group(inputs):
        rows_coords, rows_panel, rows_list = inputs
        kernel = cov_blocks(rows_coords, wide_coords[rows_list], ranges, period)
        product = jnp.einsum(
            "gnab,gnbc->gac", kernel, wide_panel[rows_list], preferred_element_type=jnp.float32
        )
        return product + NUGGET * rows_panel.astype(jnp.float32)

    image = lax.map(
        one_group,
        (
            home_coords.reshape(turns, group, 3, block_size),
            blocked.reshape(turns, group, block_size, width),
            local_column.reshape(turns, group, -1),
        ),
    )
    image = image.reshape(block_count * block_size, width)
    total_cells = jnp.float32(image.shape[0] * sector_count * slab_count)
    local_gram = (
        jnp.dot(image.T, image, precision=lax.Precision.HIGHEST, preferred_element_type=jnp.float32)
        / total_cells
    )
    lower = jnp.linalg.cholesky(lax.psum(local_gram, ("sector", "depth")))
    inverse = jax.scipy.linalg.solve_triangular(
        lower, jnp.eye(width, dtype=jnp.float32), lower=True
    )
    basis = jnp.dot(
        image, inverse.T, precision=lax.Precision.HIGHEST, preferred_element_type=jnp.float32
    )
    return (basis, lower.T)


def solution(mesh):
    in_specs = (
        P(("sector", "depth"), None),
        P(None, ("sector", "depth")),
        P(("sector", "depth"), None),
        P(),
    )
    out_specs = (P(("sector", "depth"), None), P())
    return jax.shard_map(
        on_device, mesh=mesh, in_specs=in_specs, out_specs=out_specs, check_vma=False
    )
```

profile of v0, /device:TPU:1, one launch (start us, length us, event | category | flops | bytes accessed | tf_op | source)
XLA Modules:
  0.0 625.7 jit_solution(4741672495982144289)
XLA Ops:
  7.2 4.2 collective-permute-start.4
  11.4 3.2 collective-permute-start
  14.7 1.2 collective-permute-start.2
  15.9 15.5 %collective-permute-done = s32[3,4096]{1,0:T(4,128)S(1)} collective-permute-done((s32[3,4096]{1,0:T(4,128)}, s32[3,4096]{1,0:T(4,128)S(1)}, u32[]{:S(2)}, u32[]{:S(2)}) %collective-permute-start) | collective-permute-done | bytes 49184 | tf_op jit(solution)/shard_map/ppermute | solution.py:14
  31.4 3.9 collective-permute-start.1
  36.0 1.9 collective-permute-done.2
  38.0 2.1 collective-permute-start.3
  40.1 1.2 collective-permute-start.5
  41.3 5.5 collective-permute-start.7
  46.8 0.8 constant_dynamic-update-slice_fusion
  47.9 8.0 %collective-permute-done.5 = bf16[32,128,128]{2,1,0:T(8,128)(2,1)S(1)} collective-permute-done((bf16[32,128,128]{2,1,0:T(8,128)(2,1)}, bf16[32,128,128]{2,1,0:T(8,128)(2,1)S(1)}, u32[]{:S(2)}, u32[]{:S(2)}) %collective-permute-start.5) | collective-permute-done | bytes 1048608 | tf_op jit(solution)/shard_map/ppermute | solution.py:14
  56.0 1.4 constant_dynamic-update-slice_fusion.4
  57.5 1.4 constant_dynamic-update-slice_fusion.2
  59.0 9.7 %collective-permute-done.7 = bf16[32,128,128]{2,1,0:T(8,128)(2,1)S(1)} collective-permute-done((bf16[32,128,128]{2,1,0:T(8,128)(2,1)}, bf16[32,128,128]{2,1,0:T(8,128)(2,1)S(1)}, u32[]{:S(2)}, u32[]{:S(2)}) %collective-permute-start.7) | collective-permute-done | bytes 1048608 | tf_op jit(solution)/shard_map/ppermute | solution.py:14
  68.8 2.4 copy-done
  71.2 272.4 %while.10 = (s32[]{:T(128)}, f32[8,4,128,128]{3,2,1,0:T(8,128)S(1)}, s32[8,4,3,128]{3,1,0,2:T(4,128)S(1)}, s32[8,4,32]{2,1,0:T(4,128)S(1)}, s32[160,3,128]{2,1,0...) while((s32[]{:T(128)}, ...), condition=%wide.region_1.2_spmd, body=%wide.region_0.1_spmd.sunk | while | flops 589497728 | bytes 68511408 | solution.py:78
  72.1 11.8 %subtract_convert_fusion.2 = f32[4,32,3,128,128]{4,3,1,0,2:T(8,128)} fusion(s32[4,32,3,128]{3,1,0,2:T(8,128)S(1)} %copy.35, s32[4,3,128]{2,0,1:T(4,128)S(1)} %dynamic-slice_bitcast_fusion.2), kind=kLoop, calls=%fused_computation.2.clone.1 | loop fusion | flops 12582912 | bytes 25368576 | tf_op jit(solution)/shard_map/while/body/eval_jaxpr/convert_element_type | solution.py:26
  84.0 5.6 gather_fusion
  90.2 15.0 %fusion.56 = f32[8,4,128,128]{3,2,1,0:T(8,128)S(1)} fusion(f32[8,4,128,128]{3,2,1,0:T(8,128)S(1)} %get-tuple-element.145, s32[]{:T(128)} %get-tuple-element.144, bf16[4,32,128,128]{3,2,1,0:T(8,128)(2,1)} %bitcast.145, f32[4,32,3,128,128]{4,3,1,0,2:T(8,128)} %subtract_convert_fusion.2, f32[]{:T(128)} %bitcast.142, f32[]{:T(128)} %bitcast.143, ...), kind=kOutput, calls=%fused_computation.23.clone.1 | convolution fusion | flops 576913408 | bytes 29753360 | tf_op jit(solution)/shard_map/while/body/eval_jaxpr/gnab,gnbc->gac/dot_general | solution.py:73
  106.2 11.8 %subtract_convert_fusion.2 = f32[4,32,3,128,128]{4,3,1,0,2:T(8,128)} fusion(s32[4,32,3,128]{3,1,0,2:T(8,128)S(1)} %copy.35, s32[4,3,128]{2,0,1:T(4,128)S(1)} %dynamic-slice_bitcast_fusion.2), kind=kLoop, calls=%fused_computation.2.clone.1 | loop fusion | flops 12582912 | bytes 25368576 | tf_op jit(solution)/shard_map/while/body/eval_jaxpr/convert_element_type | solution.py:26
  118.0 5.6 gather_fusion
  124.2 15.0 %fusion.56 = f32[8,4,128,128]{3,2,1,0:T(8,128)S(1)} fusion(f32[8,4,128,128]{3,2,1,0:T(8,128)S(1)} %get-tuple-element.145, s32[]{:T(128)} %get-tuple-element.144, bf16[4,32,128,128]{3,2,1,0:T(8,128)(2,1)} %bitcast.145, f32[4,32,3,128,128]{4,3,1,0,2:T(8,128)} %subtract_convert_fusion.2, f32[]{:T(128)} %bitcast.142, f32[]{:T(128)} %bitcast.143, ...), kind=kOutput, calls=%fused_computation.23.clone.1 | convolution fusion | flops 576913408 | bytes 29753360 | tf_op jit(solution)/shard_map/while/body/eval_jaxpr/gnab,gnbc->gac/dot_general | solution.py:73
  139.4 0.8 gather_fusion.1
  140.2 11.8 %subtract_convert_fusion.2 = f32[4,32,3,128,128]{4,3,1,0,2:T(8,128)} fusion(s32[4,32,3,128]{3,1,0,2:T(8,128)S(1)} %copy.35, s32[4,3,128]{2,0,1:T(4,128)S(1)} %dynamic-slice_bitcast_fusion.2), kind=kLoop, calls=%fused_computation.2.clone.1 | loop fusion | flops 12582912 | bytes 25368576 | tf_op jit(solution)/shard_map/while/body/eval_jaxpr/convert_element_type | solution.py:26
  152.0 5.6 gather_fusion
  158.3 15.0 %fusion.56 = f32[8,4,128,128]{3,2,1,0:T(8,128)S(1)} fusion(f32[8,4,128,128]{3,2,1,0:T(8,128)S(1)} %get-tuple-element.145, s32[]{:T(128)} %get-tuple-element.144, bf16[4,32,128,128]{3,2,1,0:T(8,128)(2,1)} %bitcast.145, f32[4,32,3,128,128]{4,3,1,0,2:T(8,128)} %subtract_convert_fusion.2, f32[]{:T(128)} %bitcast.142, f32[]{:T(128)} %bitcast.143, ...), kind=kOutput, calls=%fused_computation.23.clone.1 | convolution fusion | flops 576913408 | bytes 29753360 | tf_op jit(solution)/shard_map/while/body/eval_jaxpr/gnab,gnbc->gac/dot_general | solution.py:73
  174.2 11.8 %subtract_convert_fusion.2 = f32[4,32,3,128,128]{4,3,1,0,2:T(8,128)} fusion(s32[4,32,3,128]{3,1,0,2:T(8,128)S(1)} %copy.35, s32[4,3,128]{2,0,1:T(4,128)S(1)} %dynamic-slice_bitcast_fusion.2), kind=kLoop, calls=%fused_computation.2.clone.1 | loop fusion | flops 12582912 | bytes 25368576 | tf_op jit(solution)/shard_map/while/body/eval_jaxpr/convert_element_type | solution.py:26
  186.0 5.6 gather_fusion
  192.3 15.0 %fusion.56 = f32[8,4,128,128]{3,2,1,0:T(8,128)S(1)} fusion(f32[8,4,128,128]{3,2,1,0:T(8,128)S(1)} %get-tuple-element.145, s32[]{:T(128)} %get-tuple-element.144, bf16[4,32,128,128]{3,2,1,0:T(8,128)(2,1)} %bitcast.145, f32[4,32,3,128,128]{4,3,1,0,2:T(8,128)} %subtract_convert_fusion.2, f32[]{:T(128)} %bitcast.142, f32[]{:T(128)} %bitcast.143, ...), kind=kOutput, calls=%fused_computation.23.clone.1 | convolution fusion | flops 576913408 | bytes 29753360 | tf_op jit(solution)/shard_map/while/body/eval_jaxpr/gnab,gnbc->gac/dot_general | solution.py:73
  208.2 11.8 %subtract_convert_fusion.2 = f32[4,32,3,128,128]{4,3,1,0,2:T(8,128)} fusion(s32[4,32,3,128]{3,1,0,2:T(8,128)S(1)} %copy.35, s32[4,3,128]{2,0,1:T(4,128)S(1)} %dynamic-slice_bitcast_fusion.2), kind=kLoop, calls=%fused_computation.2.clone.1 | loop fusion | flops 12582912 | bytes 25368576 | tf_op jit(solution)/shard_map/while/body/eval_jaxpr/convert_element_type | solution.py:26
  220.1 5.6 gather_fusion
  226.3 15.0 %fusion.56 = f32[8,4,128,128]{3,2,1,0:T(8,128)S(1)} fusion(f32[8,4,128,128]{3,2,1,0:T(8,128)S(1)} %get-tuple-element.145, s32[]{:T(128)} %get-tuple-element.144, bf16[4,32,128,128]{3,2,1,0:T(8,128)(2,1)} %bitcast.145, f32[4,32,3,128,128]{4,3,1,0,2:T(8,128)} %subtract_convert_fusion.2, f32[]{:T(128)} %bitcast.142, f32[]{:T(128)} %bitcast.143, ...), kind=kOutput, calls=%fused_computation.23.clone.1 | convolution fusion | flops 576913408 | bytes 29753360 | tf_op jit(solution)/shard_map/while/body/eval_jaxpr/gnab,gnbc->gac/dot_general | solution.py:73
  242.3 11.8 %subtract_convert_fusion.2 = f32[4,32,3,128,128]{4,3,1,0,2:T(8,128)} fusion(s32[4,32,3,128]{3,1,0,2:T(8,128)S(1)} %copy.35, s32[4,3,128]{2,0,1:T(4,128)S(1)} %dynamic-slice_bitcast_fusion.2), kind=kLoop, calls=%fused_computation.2.clone.1 | loop fusion | flops 12582912 | bytes 25368576 | tf_op jit(solution)/shard_map/while/body/eval_jaxpr/convert_element_type | solution.py:26
  254.1 5.6 gather_fusion
  260.3 15.0 %fusion.56 = f32[8,4,128,128]{3,2,1,0:T(8,128)S(1)} fusion(f32[8,4,128,128]{3,2,1,0:T(8,128)S(1)} %get-tuple-element.145, s32[]{:T(128)} %get-tuple-element.144, bf16[4,32,128,128]{3,2,1,0:T(8,128)(2,1)} %bitcast.145, f32[4,32,3,128,128]{4,3,1,0,2:T(8,128)} %subtract_convert_fusion.2, f32[]{:T(128)} %bitcast.142, f32[]{:T(128)} %bitcast.143, ...), kind=kOutput, calls=%fused_computation.23.clone.1 | convolution fusion | flops 576913408 | bytes 29753360 | tf_op jit(solution)/shard_map/while/body/eval_jaxpr/gnab,gnbc->gac/dot_general | solution.py:73
  276.3 11.8 %subtract_convert_fusion.2 = f32[4,32,3,128,128]{4,3,1,0,2:T(8,128)} fusion(s32[4,32,3,128]{3,1,0,2:T(8,128)S(1)} %copy.35, s32[4,3,128]{2,0,1:T(4,128)S(1)} %dynamic-slice_bitcast_fusion.2), kind=kLoop, calls=%fused_computation.2.clone.1 | loop fusion | flops 12582912 | bytes 25368576 | tf_op jit(solution)/shard_map/while/body/eval_jaxpr/convert_element_type | solution.py:26
  288.1 5.6 gather_fusion
  294.4 15.0 %fusion.56 = f32[8,4,128,128]{3,2,1,0:T(8,128)S(1)} fusion(f32[8,4,128,128]{3,2,1,0:T(8,128)S(1)} %get-tuple-element.145, s32[]{:T(128)} %get-tuple-element.144, bf16[4,32,128,128]{3,2,1,0:T(8,128)(2,1)} %bitcast.145, f32[4,32,3,128,128]{4,3,1,0,2:T(8,128)} %subtract_convert_fusion.2, f32[]{:T(128)} %bitcast.142, f32[]{:T(128)} %bitcast.143, ...), kind=kOutput, calls=%fused_computation.23.clone.1 | convolution fusion | flops 576913408 | bytes 29753360 | tf_op jit(solution)/shard_map/while/body/eval_jaxpr/gnab,gnbc->gac/dot_general | solution.py:73
  310.3 11.8 %subtract_convert_fusion.2 = f32[4,32,3,128,128]{4,3,1,0,2:T(8,128)} fusion(s32[4,32,3,128]{3,1,0,2:T(8,128)S(1)} %copy.35, s32[4,3,128]{2,0,1:T(4,128)S(1)} %dynamic-slice_bitcast_fusion.2), kind=kLoop, calls=%fused_computation.2.clone.1 | loop fusion | flops 12582912 | bytes 25368576 | tf_op jit(solution)/shard_map/while/body/eval_jaxpr/convert_element_type | solution.py:26
  322.1 5.6 gather_fusion
  328.4 15.0 %fusion.56 = f32[8,4,128,128]{3,2,1,0:T(8,128)S(1)} fusion(f32[8,4,128,128]{3,2,1,0:T(8,128)S(1)} %get-tuple-element.145, s32[]{:T(128)} %get-tuple-element.144, bf16[4,32,128,128]{3,2,1,0:T(8,128)(2,1)} %bitcast.145, f32[4,32,3,128,128]{4,3,1,0,2:T(8,128)} %subtract_convert_fusion.2, f32[]{:T(128)} %bitcast.142, f32[]{:T(128)} %bitcast.143, ...), kind=kOutput, calls=%fused_computation.23.clone.1 | convolution fusion | flops 576913408 | bytes 29753360 | tf_op jit(solution)/shard_map/while/body/eval_jaxpr/gnab,gnbc->gac/dot_general | solution.py:73
  343.6 4.1 fusion.30
  347.8 242.3 %all-reduce.2.cloned.1.call-done = f32[128,128]{0,1:T(8,128)} async-done(((f32[128,128]{0,1:T(8,128)}), f32[128,128]{0,1:T(8,128)}) %all-reduce.2.cloned.1.call-update) | async-done | bytes 65552 | tf_op jit(solution)/shard_map/psum | solution.py:92
  590.1 0.9 copy.16
  591.0 0.9 fusion.33
  591.8 11.7 %cholesky.17 = f32[128,128]{1,0:T(8,128)S(1)} custom-call(f32[128,128]{1,0:T(8,128)S(1)} %fusion.33), custom_call_target="Cholesky" | custom-call | tf_op jit(solution)/shard_map/jit(cholesky)/cholesky | solution.py:92
  604.9 9.8 %custom-call.7 = f32[1,128,128]{1,2,0:T(8,128)S(1)} custom-call(f32[1,128,128]{2,1,0:T(8,128)S(1)} %get-tuple-element.79), custom_call_target="InvertDiagBlocksLowerTriangular" | custom-call | tf_op jit(solution)/shard_map/jit(_solve_triangular)/triangular_solve | solution.py:93
  615.7 3.1 fusion.43
  (98 shorter events, 15.3 us)
Async XLA Ops:
  7.2 50.2 %copy-start.1 = (bf16[4096,128]{1,0:T(8,128)(2,1)S(1)}, bf16[4096,128]{1,0:T(8,128)(2,1)}, u32[]{:S(2)}) copy-start(bf16[4096,128]{1,0:T(8,128)(2,1)} %param.6) | copy-start | bytes 3145732
  7.2 582.9 %all-reduce.2.cloned.1.call-start = ((), (), s32[]{:S(2)}) async-start(), calls=%async_computation | async-start | bytes 131072 | tf_op jit(solution)/shard_map/psum | solution.py:92
  7.2 32.9 %collective-permute-start.4 = (bf16[32,128,128]{2,1,0:T(8,128)(2,1)}, bf16[32,128,128]{2,1,0:T(8,128)(2,1)}, u32[]{:S(2)}, u32[]{:S(2)}) collective-permute-start(bf16[32,128,128]{2,1,0:T(8,128)(2,1)} %bitcast.148), channel_id=1, source_target_pairs={{240,0},{0,16},{16,32},{32,48},{48,64},{64,80},{80,96},{96,112},{1... | collective-permute-start | bytes 3145736 | tf_op jit(solution)/shard_map/ppermute | solution.py:14
  11.4 29.8 %collective-permute-start.6 = (bf16[32,128,128]{2,1,0:T(8,128)(2,1)}, bf16[32,128,128]{2,1,0:T(8,128)(2,1)}, u32[]{:S(2)}, u32[]{:S(2)}) collective-permute-start(bf16[32,128,128]{2,1,0:T(8,128)(2,1)} %bitcast.149), channel_id=1, source_target_pairs={{16,0},{32,16},{48,32},{64,48},{80,64},{96,80},{112,96},{128,112},... | collective-permute-start | bytes 3145736 | tf_op jit(solution)/shard_map/ppermute | solution.py:14
  11.4 20.0 %collective-permute-start = (s32[3,4096]{1,0:T(4,128)}, s32[3,4096]{1,0:T(4,128)S(1)}, u32[]{:S(2)}, u32[]{:S(2)}) collective-permute-start(s32[3,4096]{1,0:T(4,128)} %param.7), channel_id=1, source_target_pairs={{240,0},{0,16},{16,32},{32,48},{48,64},{64,80},{80,96},{96,112},{1... | collective-permute-start | bytes 147464 | tf_op jit(solution)/shard_map/ppermute | solution.py:14
  14.7 23.3 %collective-permute-start.2 = (s32[3,4096]{1,0:T(4,128)}, s32[3,4096]{1,0:T(4,128)S(1)}, u32[]{:S(2)}, u32[]{:S(2)}) collective-permute-start(s32[3,4096]{1,0:T(4,128)} %param.7), channel_id=1, source_target_pairs={{16,0},{32,16},{48,32},{64,48},{80,64},{96,80},{112,96},{128,112},... | collective-permute-start | bytes 147464 | tf_op jit(solution)/shard_map/ppermute | solution.py:14
  31.4 9.8 %collective-permute-start.1 = (s32[3,4096]{1,0:T(4,128)S(1)}, s32[3,4096]{1,0:T(4,128)S(1)}, u32[]{:S(2)}, u32[]{:S(2)}) collective-permute-start(s32[3,4096]{1,0:T(4,128)S(1)} %collective-permute-done), channel_id=1, source_target_pairs={{240,0},{0,16},{16,32},{32,48},{48,64},{64,80},{80,96},{96,112},{1... | collective-permute-start | bytes 147464 | tf_op jit(solution)/shard_map/ppermute | solution.py:14
  38.0 9.7 %collective-permute-start.3 = (s32[3,4096]{1,0:T(4,128)S(1)}, s32[3,4096]{1,0:T(4,128)S(1)}, u32[]{:S(2)}, u32[]{:S(2)}) collective-permute-start(s32[3,4096]{1,0:T(4,128)S(1)} %collective-permute-done.2), channel_id=1, source_target_pairs={{16,0},{32,16},{48,32},{64,48},{80,64},{96,80},{112,96},{128,112},... | collective-permute-start | bytes 147464 | tf_op jit(solution)/shard_map/ppermute | solution.py:14
  40.1 15.8 %collective-permute-start.5 = (bf16[32,128,128]{2,1,0:T(8,128)(2,1)}, bf16[32,128,128]{2,1,0:T(8,128)(2,1)S(1)}, u32[]{:S(2)}, u32[]{:S(2)}) collective-permute-start(bf16[32,128,128]{2,1,0:T(8,128)(2,1)} %collective-permute-done.4), channel_id=1, source_target_pairs={{240,0},{0,16},{16,32},{32,48},{48,64},{64,80},{80,96},{96,112},{1... | collective-permute-start | bytes 3145736 | tf_op jit(solution)/shard_map/ppermute | solution.py:14
  41.3 27.4 %collective-permute-start.7 = (bf16[32,128,128]{2,1,0:T(8,128)(2,1)}, bf16[32,128,128]{2,1,0:T(8,128)(2,1)S(1)}, u32[]{:S(2)}, u32[]{:S(2)}) collective-permute-start(bf16[32,128,128]{2,1,0:T(8,128)(2,1)} %collective-permute-done.6), channel_id=1, source_target_pairs={{16,0},{32,16},{48,32},{64,48},{80,64},{96,80},{112,96},{128,112},... | collective-permute-start | bytes 3145736 | tf_op jit(solution)/shard_map/ppermute | solution.py:14
  47.9 23.4 %copy-start.3 = (f32[3]{0:T(128)S(1)}, f32[3]{0:T(128)}, u32[]{:S(2)}) copy-start(f32[3]{0:T(128)} %param.9) | copy-start | bytes 40
  68.8 2.4 copy-start
  84.0 6.3 %copy-start.2 = (bf16[4096,128]{1,0:T(8,128)(2,1)S(1)}, bf16[4096,128]{1,0:T(8,128)(2,1)}, u32[]{:S(2)}) copy-start(bf16[4096,128]{1,0:T(8,128)(2,1)} %get-tuple-element.174) | copy-start | bytes 3145732 | tf_op jit(solution)/shard_map/while
  118.0 6.3 %copy-start.2 = (bf16[4096,128]{1,0:T(8,128)(2,1)S(1)}, bf16[4096,128]{1,0:T(8,128)(2,1)}, u32[]{:S(2)}) copy-start(bf16[4096,128]{1,0:T(8,128)(2,1)} %get-tuple-element.174) | copy-start | bytes 3145732 | tf_op jit(solution)/shard_map/while
  152.0 6.3 %copy-start.2 = (bf16[4096,128]{1,0:T(8,128)(2,1)S(1)}, bf16[4096,128]{1,0:T(8,128)(2,1)}, u32[]{:S(2)}) copy-start(bf16[4096,128]{1,0:T(8,128)(2,1)} %get-tuple-element.174) | copy-start | bytes 3145732 | tf_op jit(solution)/shard_map/while
  186.0 6.3 %copy-start.2 = (bf16[4096,128]{1,0:T(8,128)(2,1)S(1)}, bf16[4096,128]{1,0:T(8,128)(2,1)}, u32[]{:S(2)}) copy-start(bf16[4096,128]{1,0:T(8,128)(2,1)} %get-tuple-element.174) | copy-start | bytes 3145732 | tf_op jit(solution)/shard_map/while
  220.1 6.3 %copy-start.2 = (bf16[4096,128]{1,0:T(8,128)(2,1)S(1)}, bf16[4096,128]{1,0:T(8,128)(2,1)}, u32[]{:S(2)}) copy-start(bf16[4096,128]{1,0:T(8,128)(2,1)} %get-tuple-element.174) | copy-start | bytes 3145732 | tf_op jit(solution)/shard_map/while
  254.1 6.3 %copy-start.2 = (bf16[4096,128]{1,0:T(8,128)(2,1)S(1)}, bf16[4096,128]{1,0:T(8,128)(2,1)}, u32[]{:S(2)}) copy-start(bf16[4096,128]{1,0:T(8,128)(2,1)} %get-tuple-element.174) | copy-start | bytes 3145732 | tf_op jit(solution)/shard_map/while
  288.1 6.3 %copy-start.2 = (bf16[4096,128]{1,0:T(8,128)(2,1)S(1)}, bf16[4096,128]{1,0:T(8,128)(2,1)}, u32[]{:S(2)}) copy-start(bf16[4096,128]{1,0:T(8,128)(2,1)} %get-tuple-element.174) | copy-start | bytes 3145732 | tf_op jit(solution)/shard_map/while
  322.1 6.3 %copy-start.2 = (bf16[4096,128]{1,0:T(8,128)(2,1)S(1)}, bf16[4096,128]{1,0:T(8,128)(2,1)}, u32[]{:S(2)}) copy-start(bf16[4096,128]{1,0:T(8,128)(2,1)} %get-tuple-element.174) | copy-start | bytes 3145732 | tf_op jit(solution)/shard_map/while
Sparse Core Ops, SparseCore 0:
  347.9 242.1 all-reduce.1
where the time goes:
time: 626 us
  waiting for transfers between devices  278 us (44%)
  matrix products  128 us (20%)
  other arithmetic  119 us (19%)
  local copies, waits for them, and re-layouts  65.2 us (10%)
  starting transfers between devices  21.4 us (3%)
  between operations  14.2 us (2%)
    psum x1, waiting for transfers between devices, on_device(): lower = jnp.linalg.cholesky(lax.psum(local_gram, ('sector', 'depth')))  242 us
    dot_general x8, matrix products, one_group(): jnp.einsum('gnab,gnbc->gac', kernel, wide_panel[rows_list], preferred_ele...  120 us
    convert_element_type x8, other arithmetic, cov_blocks(): (home[:, None, :, :, None] - remote[:, :, :, None, :]).astype(jnp.float32)  94.5 us
    gather x8, local copies, waits for them, and re-layouts, one_group(): wide_panel[rows_list]  44.8 us
    ppermute x8, waiting for transfers between devices, passed_along(): return lax.ppermute(block, axis, route)  35.2 us
    ppermute x8, starting transfers between devices, passed_along(): return lax.ppermute(block, axis, route)  21.3 us
  transfers between devices with their start and end apart: 9, of which 5 were waited for; matrix products, arithmetic and copies ran while one was open for 1% of the time, Pallas kernels for 0%

commit v1 on v0

--- a/solution.py
+++ b/solution.py
@@ -89,7 +89,7 @@
         jnp.dot(image.T, image, precision=lax.Precision.HIGHEST, preferred_element_type=jnp.float32)
         / total_cells
     )
-    lower = jnp.linalg.cholesky(lax.psum(local_gram, ("sector", "depth")))
+    lower = jnp.linalg.cholesky(jnp.sum(lax.all_gather(local_gram, ("sector", "depth")), axis=0))
     inverse = jax.scipy.linalg.solve_triangular(
         lower, jnp.eye(width, dtype=jnp.float32), lower=True
     )

time: 626 us -> 1130 us (1.81)
  waiting for transfers between devices: 278 us -> 771 us
    all_gather x0 -> x1, waiting for transfers between devices: none -> 736 us  [on_device(): lax.all_gather(local_gram, ('sector', 'depth'))]
    psum x1 -> x0, waiting for transfers between devices: 242 us -> none  [on_device(): lower = jnp.linalg.cholesky(lax.psum(local_gram, ('sector', 'depth')))]
  transfers between devices with their start and end apart: 9 -> 9, of which waited for: 5 -> 5; matrix products, arithmetic and copies ran while one was open for 1% -> 0% of each run, Pallas kernels for 0% -> 0%
where the time goes in v1:
time: 1130 us
  waiting for transfers between devices  771 us (68%)
  matrix products  132 us (12%)
  other arithmetic  125 us (11%)
  local copies, waits for them, and re-layouts  63.7 us (6%)
  starting transfers between devices  21.4 us (2%)
  between operations  14.2 us (1%)
    all_gather x1, waiting for transfers between devices, on_device(): lax.all_gather(local_gram, ('sector', 'depth'))  736 us
    dot_general x8, matrix products, one_group(): jnp.einsum('gnab,gnbc->gac', kernel, wide_panel[rows_list], preferred_ele...  124 us
    convert_element_type x8, other arithmetic, cov_blocks(): (home[:, None, :, :, None] - remote[:, :, :, None, :]).astype(jnp.float32)  94.5 us
    gather x8, local copies, waits for them, and re-layouts, one_group(): wide_panel[rows_list]  44.1 us
    ppermute x8, waiting for transfers between devices, passed_along(): return lax.ppermute(block, axis, route)  35.2 us
  transfers between devices with their start and end apart: 9, of which 5 were waited for; matrix products, arithmetic and copies ran while one was open for 0% of the time, Pallas kernels for 0%

profile of v1, /device:TPU:1, one launch (start us, length us, event | category | flops | bytes accessed | tf_op | source)
XLA Modules:
  0.0 1127.4 jit_solution(10961353376852539779)
XLA Ops:
  7.2 4.2 collective-permute-start.4
  11.4 3.2 collective-permute-start
  14.7 1.2 collective-permute-start.2
  15.9 15.5 %collective-permute-done = s32[3,4096]{1,0:T(4,128)S(1)} collective-permute-done((s32[3,4096]{1,0:T(4,128)}, s32[3,4096]{1,0:T(4,128)S(1)}, u32[]{:S(2)}, u32[]{:S(2)}) %collective-permute-start) | collective-permute-done | bytes 49184 | tf_op jit(solution)/shard_map/ppermute | solution.py:14
  31.4 3.9 collective-permute-start.1
  36.0 1.9 collective-permute-done.2
  38.0 2.1 collective-permute-start.3
  40.1 1.2 collective-permute-start.5
  41.3 5.5 collective-permute-start.7
  46.8 0.8 constant_dynamic-update-slice_fusion
  47.9 8.0 collective-permute-done.5
  56.0 1.4 constant_dynamic-update-slice_fusion.4
  57.5 1.4 constant_dynamic-update-slice_fusion.2
  58.9 9.8 collective-permute-done.7
  68.8 2.4 copy-done
  71.2 275.9 %while.10 = (s32[]{:T(128)}, f32[8,4,128,128]{3,2,1,0:T(8,128)S(1)}, s32[8,4,3,128]{3,1,0,2:T(4,128)S(1)}, s32[8,4,32]{2,1,0:T(4,128)S(1)}, s32[160,3,128]{2,1,0...) while((s32[]{:T(128)}, ...), condition=%wide.region_1.2_spmd, body=%wide.region_0.1_spmd.sunk | while | flops 589497728 | bytes 64317068 | solution.py:78
  72.1 11.8 %subtract_convert_fusion.2 = f32[4,32,3,128,128]{4,3,1,0,2:T(8,128)} fusion(s32[4,32,3,128]{3,1,0,2:T(8,128)S(1)} %copy.38, s32[4,3,128]{2,0,1:T(4,128)S(1)} %dynamic-slice_bitcast_fusion.2), kind=kLoop, calls=%fused_computation.2.clone.1 | loop fusion | flops 12582912 | bytes 25368576 | tf_op jit(solution)/shard_map/while/body/eval_jaxpr/convert_element_type | solution.py:26
  83.9 5.5 gather_fusion
  90.1 15.5 %fusion.56 = f32[8,4,128,128]{3,2,1,0:T(8,128)S(1)} fusion(f32[8,4,128,128]{3,2,1,0:T(8,128)S(1)} %get-tuple-element.155, s32[]{:T(128)} %get-tuple-element.154, bf16[4,32,128,128]{3,2,1,0:T(8,128)(2,1)} %bitcast.148, f32[4,32,3,128,128]{4,3,1,0,2:T(8,128)} %subtract_convert_fusion.2, f32[]{:T(128)} %bitcast.145, f32[]{:T(128)} %bitcast.146, ...), kind=kOutput, calls=%fused_computation.23.clone.1 | convolution fusion | flops 576913408 | bytes 29753360 | tf_op jit(solution)/shard_map/while/body/eval_jaxpr/gnab,gnbc->gac/dot_general | solution.py:73
  106.6 11.8 %subtract_convert_fusion.2 = f32[4,32,3,128,128]{4,3,1,0,2:T(8,128)} fusion(s32[4,32,3,128]{3,1,0,2:T(8,128)S(1)} %copy.38, s32[4,3,128]{2,0,1:T(4,128)S(1)} %dynamic-slice_bitcast_fusion.2), kind=kLoop, calls=%fused_computation.2.clone.1 | loop fusion | flops 12582912 | bytes 25368576 | tf_op jit(solution)/shard_map/while/body/eval_jaxpr/convert_element_type | solution.py:26
  118.4 5.5 gather_fusion
  124.6 15.5 %fusion.56 = f32[8,4,128,128]{3,2,1,0:T(8,128)S(1)} fusion(f32[8,4,128,128]{3,2,1,0:T(8,128)S(1)} %get-tuple-element.155, s32[]{:T(128)} %get-tuple-element.154, bf16[4,32,128,128]{3,2,1,0:T(8,128)(2,1)} %bitcast.148, f32[4,32,3,128,128]{4,3,1,0,2:T(8,128)} %subtract_convert_fusion.2, f32[]{:T(128)} %bitcast.145, f32[]{:T(128)} %bitcast.146, ...), kind=kOutput, calls=%fused_computation.23.clone.1 | convolution fusion | flops 576913408 | bytes 29753360 | tf_op jit(solution)/shard_map/while/body/eval_jaxpr/gnab,gnbc->gac/dot_general | solution.py:73
  140.3 0.8 gather_fusion.1
  141.1 11.8 %subtract_convert_fusion.2 = f32[4,32,3,128,128]{4,3,1,0,2:T(8,128)} fusion(s32[4,32,3,128]{3,1,0,2:T(8,128)S(1)} %copy.38, s32[4,3,128]{2,0,1:T(4,128)S(1)} %dynamic-slice_bitcast_fusion.2), kind=kLoop, calls=%fused_computation.2.clone.1 | loop fusion | flops 12582912 | bytes 25368576 | tf_op jit(solution)/shard_map/while/body/eval_jaxpr/convert_element_type | solution.py:26
  152.9 5.5 gather_fusion
  159.1 15.5 %fusion.56 = f32[8,4,128,128]{3,2,1,0:T(8,128)S(1)} fusion(f32[8,4,128,128]{3,2,1,0:T(8,128)S(1)} %get-tuple-element.155, s32[]{:T(128)} %get-tuple-element.154, bf16[4,32,128,128]{3,2,1,0:T(8,128)(2,1)} %bitcast.148, f32[4,32,3,128,128]{4,3,1,0,2:T(8,128)} %subtract_convert_fusion.2, f32[]{:T(128)} %bitcast.145, f32[]{:T(128)} %bitcast.146, ...), kind=kOutput, calls=%fused_computation.23.clone.1 | convolution fusion | flops 576913408 | bytes 29753360 | tf_op jit(solution)/shard_map/while/body/eval_jaxpr/gnab,gnbc->gac/dot_general | solution.py:73
  175.5 11.8 %subtract_convert_fusion.2 = f32[4,32,3,128,128]{4,3,1,0,2:T(8,128)} fusion(s32[4,32,3,128]{3,1,0,2:T(8,128)S(1)} %copy.38, s32[4,3,128]{2,0,1:T(4,128)S(1)} %dynamic-slice_bitcast_fusion.2), kind=kLoop, calls=%fused_computation.2.clone.1 | loop fusion | flops 12582912 | bytes 25368576 | tf_op jit(solution)/shard_map/while/body/eval_jaxpr/convert_element_type | solution.py:26
  187.3 5.5 gather_fusion
  193.5 15.5 %fusion.56 = f32[8,4,128,128]{3,2,1,0:T(8,128)S(1)} fusion(f32[8,4,128,128]{3,2,1,0:T(8,128)S(1)} %get-tuple-element.155, s32[]{:T(128)} %get-tuple-element.154, bf16[4,32,128,128]{3,2,1,0:T(8,128)(2,1)} %bitcast.148, f32[4,32,3,128,128]{4,3,1,0,2:T(8,128)} %subtract_convert_fusion.2, f32[]{:T(128)} %bitcast.145, f32[]{:T(128)} %bitcast.146, ...), kind=kOutput, calls=%fused_computation.23.clone.1 | convolution fusion | flops 576913408 | bytes 29753360 | tf_op jit(solution)/shard_map/while/body/eval_jaxpr/gnab,gnbc->gac/dot_general | solution.py:73
  210.0 11.8 %subtract_convert_fusion.2 = f32[4,32,3,128,128]{4,3,1,0,2:T(8,128)} fusion(s32[4,32,3,128]{3,1,0,2:T(8,128)S(1)} %copy.38, s32[4,3,128]{2,0,1:T(4,128)S(1)} %dynamic-slice_bitcast_fusion.2), kind=kLoop, calls=%fused_computation.2.clone.1 | loop fusion | flops 12582912 | bytes 25368576 | tf_op jit(solution)/shard_map/while/body/eval_jaxpr/convert_element_type | solution.py:26
  221.8 5.5 gather_fusion
  228.0 15.5 %fusion.56 = f32[8,4,128,128]{3,2,1,0:T(8,128)S(1)} fusion(f32[8,4,128,128]{3,2,1,0:T(8,128)S(1)} %get-tuple-element.155, s32[]{:T(128)} %get-tuple-element.154, bf16[4,32,128,128]{3,2,1,0:T(8,128)(2,1)} %bitcast.148, f32[4,32,3,128,128]{4,3,1,0,2:T(8,128)} %subtract_convert_fusion.2, f32[]{:T(128)} %bitcast.145, f32[]{:T(128)} %bitcast.146, ...), kind=kOutput, calls=%fused_computation.23.clone.1 | convolution fusion | flops 576913408 | bytes 29753360 | tf_op jit(solution)/shard_map/while/body/eval_jaxpr/gnab,gnbc->gac/dot_general | solution.py:73
  244.5 11.8 %subtract_convert_fusion.2 = f32[4,32,3,128,128]{4,3,1,0,2:T(8,128)} fusion(s32[4,32,3,128]{3,1,0,2:T(8,128)S(1)} %copy.38, s32[4,3,128]{2,0,1:T(4,128)S(1)} %dynamic-slice_bitcast_fusion.2), kind=kLoop, calls=%fused_computation.2.clone.1 | loop fusion | flops 12582912 | bytes 25368576 | tf_op jit(solution)/shard_map/while/body/eval_jaxpr/convert_element_type | solution.py:26
  256.3 5.5 gather_fusion
  262.4 15.5 %fusion.56 = f32[8,4,128,128]{3,2,1,0:T(8,128)S(1)} fusion(f32[8,4,128,128]{3,2,1,0:T(8,128)S(1)} %get-tuple-element.155, s32[]{:T(128)} %get-tuple-element.154, bf16[4,32,128,128]{3,2,1,0:T(8,128)(2,1)} %bitcast.148, f32[4,32,3,128,128]{4,3,1,0,2:T(8,128)} %subtract_convert_fusion.2, f32[]{:T(128)} %bitcast.145, f32[]{:T(128)} %bitcast.146, ...), kind=kOutput, calls=%fused_computation.23.clone.1 | convolution fusion | flops 576913408 | bytes 29753360 | tf_op jit(solution)/shard_map/while/body/eval_jaxpr/gnab,gnbc->gac/dot_general | solution.py:73
  278.1 0.8 gather_fusion.1
  278.9 11.8 %subtract_convert_fusion.2 = f32[4,32,3,128,128]{4,3,1,0,2:T(8,128)} fusion(s32[4,32,3,128]{3,1,0,2:T(8,128)S(1)} %copy.38, s32[4,3,128]{2,0,1:T(4,128)S(1)} %dynamic-slice_bitcast_fusion.2), kind=kLoop, calls=%fused_computation.2.clone.1 | loop fusion | flops 12582912 | bytes 25368576 | tf_op jit(solution)/shard_map/while/body/eval_jaxpr/convert_element_type | solution.py:26
  290.7 5.5 gather_fusion
  296.9 15.5 %fusion.56 = f32[8,4,128,128]{3,2,1,0:T(8,128)S(1)} fusion(f32[8,4,128,128]{3,2,1,0:T(8,128)S(1)} %get-tuple-element.155, s32[]{:T(128)} %get-tuple-element.154, bf16[4,32,128,128]{3,2,1,0:T(8,128)(2,1)} %bitcast.148, f32[4,32,3,128,128]{4,3,1,0,2:T(8,128)} %subtract_convert_fusion.2, f32[]{:T(128)} %bitcast.145, f32[]{:T(128)} %bitcast.146, ...), kind=kOutput, calls=%fused_computation.23.clone.1 | convolution fusion | flops 576913408 | bytes 29753360 | tf_op jit(solution)/shard_map/while/body/eval_jaxpr/gnab,gnbc->gac/dot_general | solution.py:73
  313.4 11.8 %subtract_convert_fusion.2 = f32[4,32,3,128,128]{4,3,1,0,2:T(8,128)} fusion(s32[4,32,3,128]{3,1,0,2:T(8,128)S(1)} %copy.38, s32[4,3,128]{2,0,1:T(4,128)S(1)} %dynamic-slice_bitcast_fusion.2), kind=kLoop, calls=%fused_computation.2.clone.1 | loop fusion | flops 12582912 | bytes 25368576 | tf_op jit(solution)/shard_map/while/body/eval_jaxpr/convert_element_type | solution.py:26
  325.2 5.5 gather_fusion
  331.4 15.5 %fusion.56 = f32[8,4,128,128]{3,2,1,0:T(8,128)S(1)} fusion(f32[8,4,128,128]{3,2,1,0:T(8,128)S(1)} %get-tuple-element.155, s32[]{:T(128)} %get-tuple-element.154, bf16[4,32,128,128]{3,2,1,0:T(8,128)(2,1)} %bitcast.148, f32[4,32,3,128,128]{4,3,1,0,2:T(8,128)} %subtract_convert_fusion.2, f32[]{:T(128)} %bitcast.145, f32[]{:T(128)} %bitcast.146, ...), kind=kOutput, calls=%fused_computation.23.clone.1 | convolution fusion | flops 576913408 | bytes 29753360 | tf_op jit(solution)/shard_map/while/body/eval_jaxpr/gnab,gnbc->gac/dot_general | solution.py:73
  347.2 4.1 fusion.30
  351.3 735.6 %all-gather.3.cloned.1.call-done = f32[32768,128]{1,0:T(8,128)} async-done(((f32[128,128]{1,0:T(8,128)}), f32[32768,128]{1,0:T(8,128)}) %all-gather.3.cloned.1.call-update) | async-done | bytes 16777232 | tf_op jit(solution)/shard_map/all_gather | solution.py:92
  1086.8 6.6 reduce_sum.9
  1093.5 11.7 %cholesky.17 = f32[128,128]{1,0:T(8,128)S(1)} custom-call(f32[128,128]{1,0:T(8,128)S(1)} %fusion.33), custom_call_target="Cholesky" | custom-call | tf_op jit(solution)/shard_map/jit(cholesky)/cholesky | solution.py:92
  1106.6 9.8 custom-call.7
  1117.4 3.1 fusion.43
  (83 shorter events, 14.7 us)
Async XLA Ops:
  7.2 1079.7 %all-gather.3.cloned.1.call-start = ((), (), s32[]{:S(2)}) async-start(), calls=%async_computation | async-start | bytes 16842752 | tf_op jit(solution)/shard_map/all_gather | solution.py:92
  7.2 32.9 %collective-permute-start.4 = (bf16[32,128,128]{2,1,0:T(8,128)(2,1)}, bf16[32,128,128]{2,1,0:T(8,128)(2,1)}, u32[]{:S(2)}, u32[]{:S(2)}) collective-permute-start(bf16[32,128,128]{2,1,0:T(8,128)(2,1)} %bitcast.152), channel_id=1, source_target_pairs={{240,0},{0,16},{16,32},{32,48},{48,64},{64,80},{80,96},{96,112},{1... | collective-permute-start | bytes 3145736 | tf_op jit(solution)/shard_map/ppermute | solution.py:14
  11.4 29.8 %collective-permute-start.6 = (bf16[32,128,128]{2,1,0:T(8,128)(2,1)}, bf16[32,128,128]{2,1,0:T(8,128)(2,1)}, u32[]{:S(2)}, u32[]{:S(2)}) collective-permute-start(bf16[32,128,128]{2,1,0:T(8,128)(2,1)} %bitcast.153), channel_id=1, source_target_pairs={{16,0},{32,16},{48,32},{64,48},{80,64},{96,80},{112,96},{128,112},... | collective-permute-start | bytes 3145736 | tf_op jit(solution)/shard_map/ppermute | solution.py:14
  11.4 20.0 %collective-permute-start = (s32[3,4096]{1,0:T(4,128)}, s32[3,4096]{1,0:T(4,128)S(1)}, u32[]{:S(2)}, u32[]{:S(2)}) collective-permute-start(s32[3,4096]{1,0:T(4,128)} %param.7), channel_id=1, source_target_pairs={{240,0},{0,16},{16,32},{32,48},{48,64},{64,80},{80,96},{96,112},{1... | collective-permute-start | bytes 147464 | tf_op jit(solution)/shard_map/ppermute | solution.py:14
  14.7 23.3 %collective-permute-start.2 = (s32[3,4096]{1,0:T(4,128)}, s32[3,4096]{1,0:T(4,128)S(1)}, u32[]{:S(2)}, u32[]{:S(2)}) collective-permute-start(s32[3,4096]{1,0:T(4,128)} %param.7), channel_id=1, source_target_pairs={{16,0},{32,16},{48,32},{64,48},{80,64},{96,80},{112,96},{128,112},... | collective-permute-start | bytes 147464 | tf_op jit(solution)/shard_map/ppermute | solution.py:14
  31.4 9.8 collective-permute-start.1
  36.0 21.3 %copy-start.1 = (bf16[4096,128]{1,0:T(8,128)(2,1)S(1)}, bf16[4096,128]{1,0:T(8,128)(2,1)}, u32[]{:S(2)}) copy-start(bf16[4096,128]{1,0:T(8,128)(2,1)} %param.6) | copy-start | bytes 3145732
  38.0 9.7 collective-permute-start.3
  40.1 15.8 %collective-permute-start.5 = (bf16[32,128,128]{2,1,0:T(8,128)(2,1)}, bf16[32,128,128]{2,1,0:T(8,128)(2,1)S(1)}, u32[]{:S(2)}, u32[]{:S(2)}) collective-permute-start(bf16[32,128,128]{2,1,0:T(8,128)(2,1)} %collective-permute-done.4), channel_id=1, source_target_pairs={{240,0},{0,16},{16,32},{32,48},{48,64},{64,80},{80,96},{96,112},{1... | collective-permute-start | bytes 3145736 | tf_op jit(solution)/shard_map/ppermute | solution.py:14
  41.3 27.4 %collective-permute-start.7 = (bf16[32,128,128]{2,1,0:T(8,128)(2,1)}, bf16[32,128,128]{2,1,0:T(8,128)(2,1)S(1)}, u32[]{:S(2)}, u32[]{:S(2)}) collective-permute-start(bf16[32,128,128]{2,1,0:T(8,128)(2,1)} %collective-permute-done.6), channel_id=1, source_target_pairs={{16,0},{32,16},{48,32},{64,48},{80,64},{96,80},{112,96},{128,112},... | collective-permute-start | bytes 3145736 | tf_op jit(solution)/shard_map/ppermute | solution.py:14
  47.9 23.4 %copy-start.2 = (f32[3]{0:T(128)S(1)}, f32[3]{0:T(128)}, u32[]{:S(2)}) copy-start(f32[3]{0:T(128)} %param.9) | copy-start | bytes 40
  68.8 2.4 copy-start
Sparse Core Ops, SparseCore 0:
  351.4 735.4 all-gather.2
